TPU v7x, 32 devices: a whole 2x2x4 slice. The times are simulated.
32 devices in a mesh: section: 4 (over y, x), row: 2 (over core), col: 4 (over z).
Axes of the slice: x: 2, y: 2, z: 4, core: 2. Of those that a mesh axis runs over, the one named last changes fastest.
Arguments:
- cotangent: float32 [4, 128, 4096], P('section', None, ('row', 'col')), may hold values from -6 to 6
- incoming: float32 [4, 128, 4096], P('section', None, ('row', 'col')), may hold values from -6 to 6
- upd_u: float32 [4, 8, 128, 4096], P('section', None, None, ('row', 'col')), may hold values from -4 to 4
- upd_v: float32 [4, 8, 128, 4096], P('section', None, None, ('row', 'col')), may hold values from -0.0078125 to 0.0078125
- saved_x: bfloat16 [4, 4, 128, 4096], P('section', None, None, ('row', 'col')), may hold values from -6 to 6
- saved_h: bfloat16 [4, 4, 2, 128, 14336], P('section', None, None, None, 'col'), may hold values from -6 to 6
- norm_gain: float32 [4, 4096], P('section', ('row', 'col')), may hold values from 0.25 to 1.75
- w_gate: bfloat16 [4, 4096, 14336], P('section', 'row', 'col'), may hold values from -0.09375 to 0.09375
- w_up: bfloat16 [4, 4096, 14336], P('section', 'row', 'col'), may hold values from -0.09375 to 0.09375
- w_down: bfloat16 [4, 14336, 4096], P('section', 'col', 'row'), may hold values from -0.046875 to 0.046875
Outputs:
- new_cotangent: float32 [4, 128, 4096], P('section', None, ('row', 'col'))
- residual_out: float32 [4, 128, 4096], P('section', None, ('row', 'col'))
All inputs are finite; a program needn't handle non-finite values.
Results may differ from a plain program's by a relative error of at most 0.014.
Values may be sent and summed in bfloat16 or wider, within the bound.
No kernel may reach another device: no remote copies, remote signals or barrier semaphores. Data moves between devices by JAX's collectives and lax.ppermute only.
A program may use at most 128 MiB of HBM per device.

v0:
```python
import jax
import jax.numpy as jnp
from jax import lax
from jax.sharding import PartitionSpec as P

D = 4096
eps = 1e-05


def shifted(x, axis, by):
    devices = lax.axis_size(axis)
    return lax.ppermute(x, axis, [(i, (i + by) % devices) for i in range(devices)])


def rotate(carry):
    return shifted(carry, "section", -1)


def shards(cotangent, incoming, upd_u, upd_v, saved_x, saved_h, norm_gain, w_gate, w_up, w_down):
    sections = lax.axis_size("section")
    section_idx = lax.axis_index("section")
    inputs_all = saved_x[0].astype(jnp.float32)
    hidden_all = saved_h[0]
    gain = norm_gain[0]
    wg = w_gate[0]
    wu = w_up[0]
    wd = w_down[0]

    def layer_step(step, carry):
        carry = rotate(carry)
        micro = (section_idx + step + 1) % sections
        xf = lax.dynamic_index_in_dim(inputs_all, micro, 0, keepdims=False)
        hpair = lax.dynamic_index_in_dim(hidden_all, micro, 0, keepdims=False)
        sumsq = lax.psum(jnp.sum(xf * xf, axis=1), ("row", "col"))
        gy = carry.astype(jnp.bfloat16)
        wide = lax.all_gather(gy, "col", axis=1, tiled=True)
        ga_part = lax.dot_general(
            wide, wd, (((1,), (1,)), ((), ())), preferred_element_type=jnp.float32
        )
        ga = lax.psum_scatter(ga_part, "row", scatter_dimension=1, tiled=True)
        width = ga.shape[1]
        offset = lax.axis_index("row") * width
        hg = lax.dynamic_slice_in_dim(hpair[0], offset, width, 1).astype(jnp.float32)
        hu = lax.dynamic_slice_in_dim(hpair[1], offset, width, 1).astype(jnp.float32)
        sig = jax.nn.sigmoid(hg)
        part_gate = (ga * hu * sig * (1.0 + hg * (1.0 - sig))).astype(jnp.bfloat16)
        part_up = (ga * hg * sig).astype(jnp.bfloat16)
        grad_gate, grad_up = (
            lax.all_gather(part_gate, "row", axis=1, tiled=True),
            lax.all_gather(part_up, "row", axis=1, tiled=True),
        )
        first = lax.dot_general(
            wg, grad_gate, (((1,), (1,)), ((), ())), preferred_element_type=jnp.float32
        )
        second = lax.dot_general(
            wu, grad_up, (((1,), (1,)), ((), ())), preferred_element_type=jnp.float32
        )
        normgrad = lax.psum_scatter(first + second, "col", scatter_dimension=0, tiled=True).T
        rstd = lax.rsqrt(sumsq / D + eps)[:, None]
        scaled = gain * normgrad
        inner = lax.psum(jnp.sum(scaled * xf, axis=1), ("row", "col"))[:, None] / D
        updated = carry + rstd * scaled - xf * (rstd * rstd * rstd) * inner
        active = jnp.logical_and(step >= micro, step - micro < sections)
        return jnp.where(active, updated, carry)

    pulled = lax.fori_loop(0, 2 * sections - 1, layer_step, cotangent[0])
    pulled = rotate(pulled)
    resid = pulled + incoming[0] - cotangent[0]
    local_dots = jnp.einsum("urd,rd->u", upd_v[0], resid, precision=lax.Precision.HIGHEST)
    dots = lax.psum(local_dots, ("row", "col"))
    update = jnp.einsum("u,urd->rd", dots, upd_u[0], precision=lax.Precision.HIGHEST)
    fresh = cotangent[0] + resid - update
    return (fresh[None], resid[None])


def solution(mesh):
    placed = (
        P("section", None, ("row", "col")),
        P("section", None, ("row", "col")),
        P("section", None, None, ("row", "col")),
        P("section", None, None, ("row", "col")),
        P("section", None, None, ("row", "col")),
        P("section", None, None, None, "col"),
        P("section", ("row", "col")),
        P("section", "row", "col"),
        P("section", "row", "col"),
        P("section", "col", "row"),
    )
    return jax.shard_map(
        shards,
        mesh=mesh,
        in_specs=placed,
        out_specs=(P("section", None, ("row", "col")), P("section", None, ("row", "col"))),
        check_vma=False,
    )
```

profile of v0, /device:TPU:0, one launch (start us, length us, event | category | flops | bytes accessed | tf_op | source)
XLA Modules:
  0.0 880.5 jit_solution(12553855589407518897)
XLA Ops:
  10.2 832.8 %while.15 = (s32[]{:T(128)}, f32[128,512]{1,0:T(8,128)}, s32[]{:T(128)}, f32[4,128,512]{2,1,0:T(8,128)S(1)}, f32[1,512]{1,0:T(1,128)}, /*index=5*/bf16[3584,2048...) while((s32[]{:T(128)}, f32[128,512]{1,0:T(8,128)}, ...), condition=%wide.region_7.8_spmd, body=%wide.region_0.7_spmd.sunk | while | flops 5641699840 | bytes 72765032 | solution.py:66
  20.1 15.1 %all_gather.33 = bf16[128,2048]{1,0:T(8,128)(2,1)S(1)} all-gather(bf16[128,512]{1,0:T(8,128)(2,1)S(1)} %convert_element_type.72), channel_id=1, replica_groups=mesh['section'=4,'row'=2,'col'=4] {'col'}, dimensions={1}, use_global_device_ids=true | all-gather | bytes 655360 | tf_op jit(solution)/shard_map/while/body/eval_jaxpr/all_gather | solution.py:36
  35.3 11.4 %fusion.48 = f32[128,3584]{1,0:T(8,128)} fusion(bf16[128,2048]{1,0:T(8,128)(2,1)S(1)} %all_gather.33, bf16[3584,2048]{1,0:T(8,128)(2,1)} %get-tuple-element.365), kind=kOutput, calls=%fused_computation.40.clone.1 | convolution fusion | flops 1879048192 | bytes 17039360 | tf_op jit(solution)/shard_map/while/body/eval_jaxpr/dot_general | solution.py:37
  46.7 12.0 %reduce-scatter.3.cloned.1.call-done = f32[128,1792]{1,0:T(8,128)} async-done(((f32[128,3584]{1,0:T(8,128)}), f32[128,1792]{1,0:T(8,128)}) %reduce-scatter.3.cloned.1.call-update) | async-done | bytes 917520 | tf_op jit(solution)/shard_map/while/body/eval_jaxpr/reduce_scatter | solution.py:40
  75.4 10.9 %fusion.51 = f32[2048,128]{0,1:T(8,128)} fusion(f32[128,2048]{1,0:T(8,128)S(1)} %fusion.50, bf16[128,3584]{1,0:T(8,128)(2,1)S(1)} %all_gather.35, bf16[2048,3584]{1,0:T(8,128)(2,1)} %get-tuple-element.368), kind=kOutput, calls=%fused_computation.1.clone.1 | convolution fusion | flops 1879310336 | bytes 17694720 | tf_op jit(solution)/shard_map/while/body/eval_jaxpr/dot_general | solution.py:55
  86.4 28.7 %reduce-scatter.5.cloned.1.call-done = f32[512,128]{0,1:T(8,128)} async-done(((f32[2048,128]{0,1:T(8,128)}), f32[512,128]{0,1:T(8,128)}) %reduce-scatter.5.cloned.1.call-update) | async-done | bytes 262160 | tf_op jit(solution)/shard_map/while/body/eval_jaxpr/reduce_scatter | solution.py:58
  116.2 13.7 %all-reduce.2 = (f32[128]{0:T(128)S(1)}, f32[128]{0:T(128)S(1)}) all-reduce(f32[128]{0:T(128)S(1)} %get-tuple-element.317, f32[128]{0:T(128)S(1)} %get-tuple-element.318), channel_id=1, replica_groups=mesh['section'=4,'row'=2,'col'=4] {'row','col'}, use_global_device_ids=true, to_apply=%region_6.6 | all-reduce | flops 256 | bytes 2048 | tf_op jit(solution)/shard_map/while/body/eval_jaxpr/psum | solution.py:61
  141.1 16.1 %all_gather.33 = bf16[128,2048]{1,0:T(8,128)(2,1)S(1)} all-gather(bf16[128,512]{1,0:T(8,128)(2,1)S(1)} %convert_element_type.72), channel_id=1, replica_groups=mesh['section'=4,'row'=2,'col'=4] {'col'}, dimensions={1}, use_global_device_ids=true | all-gather | bytes 655360 | tf_op jit(solution)/shard_map/while/body/eval_jaxpr/all_gather | solution.py:36
  157.2 11.3 %fusion.48 = f32[128,3584]{1,0:T(8,128)} fusion(bf16[128,2048]{1,0:T(8,128)(2,1)S(1)} %all_gather.33, bf16[3584,2048]{1,0:T(8,128)(2,1)} %get-tuple-element.365), kind=kOutput, calls=%fused_computation.40.clone.1 | convolution fusion | flops 1879048192 | bytes 17039360 | tf_op jit(solution)/shard_map/while/body/eval_jaxpr/dot_general | solution.py:37
  205.0 28.7 %reduce-scatter.5.cloned.1.call-done = f32[512,128]{0,1:T(8,128)} async-done(((f32[2048,128]{0,1:T(8,128)}), f32[512,128]{0,1:T(8,128)}) %reduce-scatter.5.cloned.1.call-update) | async-done | bytes 262160 | tf_op jit(solution)/shard_map/while/body/eval_jaxpr/reduce_scatter | solution.py:58
  234.8 13.7 %all-reduce.2 = (f32[128]{0:T(128)S(1)}, f32[128]{0:T(128)S(1)}) all-reduce(f32[128]{0:T(128)S(1)} %get-tuple-element.317, f32[128]{0:T(128)S(1)} %get-tuple-element.318), channel_id=1, replica_groups=mesh['section'=4,'row'=2,'col'=4] {'row','col'}, use_global_device_ids=true, to_apply=%region_6.6 | all-reduce | flops 256 | bytes 2048 | tf_op jit(solution)/shard_map/while/body/eval_jaxpr/psum | solution.py:61
  259.7 16.2 %all_gather.33 = bf16[128,2048]{1,0:T(8,128)(2,1)S(1)} all-gather(bf16[128,512]{1,0:T(8,128)(2,1)S(1)} %convert_element_type.72), channel_id=1, replica_groups=mesh['section'=4,'row'=2,'col'=4] {'col'}, dimensions={1}, use_global_device_ids=true | all-gather | bytes 655360 | tf_op jit(solution)/shard_map/while/body/eval_jaxpr/all_gather | solution.py:36
  275.8 11.3 %fusion.48 = f32[128,3584]{1,0:T(8,128)} fusion(bf16[128,2048]{1,0:T(8,128)(2,1)S(1)} %all_gather.33, bf16[3584,2048]{1,0:T(8,128)(2,1)} %get-tuple-element.365), kind=kOutput, calls=%fused_computation.40.clone.1 | convolution fusion | flops 1879048192 | bytes 17039360 | tf_op jit(solution)/shard_map/while/body/eval_jaxpr/dot_general | solution.py:37
  323.5 28.7 %reduce-scatter.5.cloned.1.call-done = f32[512,128]{0,1:T(8,128)} async-done(((f32[2048,128]{0,1:T(8,128)}), f32[512,128]{0,1:T(8,128)}) %reduce-scatter.5.cloned.1.call-update) | async-done | bytes 262160 | tf_op jit(solution)/shard_map/while/body/eval_jaxpr/reduce_scatter | solution.py:58
  353.3 13.7 %all-reduce.2 = (f32[128]{0:T(128)S(1)}, f32[128]{0:T(128)S(1)}) all-reduce(f32[128]{0:T(128)S(1)} %get-tuple-element.317, f32[128]{0:T(128)S(1)} %get-tuple-element.318), channel_id=1, replica_groups=mesh['section'=4,'row'=2,'col'=4] {'row','col'}, use_global_device_ids=true, to_apply=%region_6.6 | all-reduce | flops 256 | bytes 2048 | tf_op jit(solution)/shard_map/while/body/eval_jaxpr/psum | solution.py:61
  378.2 16.2 %all_gather.33 = bf16[128,2048]{1,0:T(8,128)(2,1)S(1)} all-gather(bf16[128,512]{1,0:T(8,128)(2,1)S(1)} %convert_element_type.72), channel_id=1, replica_groups=mesh['section'=4,'row'=2,'col'=4] {'col'}, dimensions={1}, use_global_device_ids=true | all-gather | bytes 655360 | tf_op jit(solution)/shard_map/while/body/eval_jaxpr/all_gather | solution.py:36
  394.4 11.3 %fusion.48 = f32[128,3584]{1,0:T(8,128)} fusion(bf16[128,2048]{1,0:T(8,128)(2,1)S(1)} %all_gather.33, bf16[3584,2048]{1,0:T(8,128)(2,1)} %get-tuple-element.365), kind=kOutput, calls=%fused_computation.40.clone.1 | convolution fusion | flops 1879048192 | bytes 17039360 | tf_op jit(solution)/shard_map/while/body/eval_jaxpr/dot_general | solution.py:37
  442.0 28.7 %reduce-scatter.5.cloned.1.call-done = f32[512,128]{0,1:T(8,128)} async-done(((f32[2048,128]{0,1:T(8,128)}), f32[512,128]{0,1:T(8,128)}) %reduce-scatter.5.cloned.1.call-update) | async-done | bytes 262160 | tf_op jit(solution)/shard_map/while/body/eval_jaxpr/reduce_scatter | solution.py:58
  471.8 13.7 %all-reduce.2 = (f32[128]{0:T(128)S(1)}, f32[128]{0:T(128)S(1)}) all-reduce(f32[128]{0:T(128)S(1)} %get-tuple-element.317, f32[128]{0:T(128)S(1)} %get-tuple-element.318), channel_id=1, replica_groups=mesh['section'=4,'row'=2,'col'=4] {'row','col'}, use_global_device_ids=true, to_apply=%region_6.6 | all-reduce | flops 256 | bytes 2048 | tf_op jit(solution)/shard_map/while/body/eval_jaxpr/psum | solution.py:61
  496.7 16.2 %all_gather.33 = bf16[128,2048]{1,0:T(8,128)(2,1)S(1)} all-gather(bf16[128,512]{1,0:T(8,128)(2,1)S(1)} %convert_element_type.72), channel_id=1, replica_groups=mesh['section'=4,'row'=2,'col'=4] {'col'}, dimensions={1}, use_global_device_ids=true | all-gather | bytes 655360 | tf_op jit(solution)/shard_map/while/body/eval_jaxpr/all_gather | solution.py:36
  512.9 11.3 %fusion.48 = f32[128,3584]{1,0:T(8,128)} fusion(bf16[128,2048]{1,0:T(8,128)(2,1)S(1)} %all_gather.33, bf16[3584,2048]{1,0:T(8,128)(2,1)} %get-tuple-element.365), kind=kOutput, calls=%fused_computation.40.clone.1 | convolution fusion | flops 1879048192 | bytes 17039360 | tf_op jit(solution)/shard_map/while/body/eval_jaxpr/dot_general | solution.py:37
  560.6 28.7 %reduce-scatter.5.cloned.1.call-done = f32[512,128]{0,1:T(8,128)} async-done(((f32[2048,128]{0,1:T(8,128)}), f32[512,128]{0,1:T(8,128)}) %reduce-scatter.5.cloned.1.call-update) | async-done | bytes 262160 | tf_op jit(solution)/shard_map/while/body/eval_jaxpr/reduce_scatter | solution.py:58
  590.4 13.7 %all-reduce.2 = (f32[128]{0:T(128)S(1)}, f32[128]{0:T(128)S(1)}) all-reduce(f32[128]{0:T(128)S(1)} %get-tuple-element.317, f32[128]{0:T(128)S(1)} %get-tuple-element.318), channel_id=1, replica_groups=mesh['section'=4,'row'=2,'col'=4] {'row','col'}, use_global_device_ids=true, to_apply=%region_6.6 | all-reduce | flops 256 | bytes 2048 | tf_op jit(solution)/shard_map/while/body/eval_jaxpr/psum | solution.py:61
  615.3 16.2 %all_gather.33 = bf16[128,2048]{1,0:T(8,128)(2,1)S(1)} all-gather(bf16[128,512]{1,0:T(8,128)(2,1)S(1)} %convert_element_type.72), channel_id=1, replica_groups=mesh['section'=4,'row'=2,'col'=4] {'col'}, dimensions={1}, use_global_device_ids=true | all-gather | bytes 655360 | tf_op jit(solution)/shard_map/while/body/eval_jaxpr/all_gather | solution.py:36
  631.5 11.3 %fusion.48 = f32[128,3584]{1,0:T(8,128)} fusion(bf16[128,2048]{1,0:T(8,128)(2,1)S(1)} %all_gather.33, bf16[3584,2048]{1,0:T(8,128)(2,1)} %get-tuple-element.365), kind=kOutput, calls=%fused_computation.40.clone.1 | convolution fusion | flops 1879048192 | bytes 17039360 | tf_op jit(solution)/shard_map/while/body/eval_jaxpr/dot_general | solution.py:37
  679.1 28.7 %reduce-scatter.5.cloned.1.call-done = f32[512,128]{0,1:T(8,128)} async-done(((f32[2048,128]{0,1:T(8,128)}), f32[512,128]{0,1:T(8,128)}) %reduce-scatter.5.cloned.1.call-update) | async-done | bytes 262160 | tf_op jit(solution)/shard_map/while/body/eval_jaxpr/reduce_scatter | solution.py:58
  708.9 13.7 %all-reduce.2 = (f32[128]{0:T(128)S(1)}, f32[128]{0:T(128)S(1)}) all-reduce(f32[128]{0:T(128)S(1)} %get-tuple-element.317, f32[128]{0:T(128)S(1)} %get-tuple-element.318), channel_id=1, replica_groups=mesh['section'=4,'row'=2,'col'=4] {'row','col'}, use_global_device_ids=true, to_apply=%region_6.6 | all-reduce | flops 256 | bytes 2048 | tf_op jit(solution)/shard_map/while/body/eval_jaxpr/psum | solution.py:61
  733.8 16.2 %all_gather.33 = bf16[128,2048]{1,0:T(8,128)(2,1)S(1)} all-gather(bf16[128,512]{1,0:T(8,128)(2,1)S(1)} %convert_element_type.72), channel_id=1, replica_groups=mesh['section'=4,'row'=2,'col'=4] {'col'}, dimensions={1}, use_global_device_ids=true | all-gather | bytes 655360 | tf_op jit(solution)/shard_map/while/body/eval_jaxpr/all_gather | solution.py:36
  750.0 11.3 %fusion.48 = f32[128,3584]{1,0:T(8,128)} fusion(bf16[128,2048]{1,0:T(8,128)(2,1)S(1)} %all_gather.33, bf16[3584,2048]{1,0:T(8,128)(2,1)} %get-tuple-element.365), kind=kOutput, calls=%fused_computation.40.clone.1 | convolution fusion | flops 1879048192 | bytes 17039360 | tf_op jit(solution)/shard_map/while/body/eval_jaxpr/dot_general | solution.py:37
  797.6 28.7 %reduce-scatter.5.cloned.1.call-done = f32[512,128]{0,1:T(8,128)} async-done(((f32[2048,128]{0,1:T(8,128)}), f32[512,128]{0,1:T(8,128)}) %reduce-scatter.5.cloned.1.call-update) | async-done | bytes 262160 | tf_op jit(solution)/shard_map/while/body/eval_jaxpr/reduce_scatter | solution.py:58
  827.4 13.7 %all-reduce.2 = (f32[128]{0:T(128)S(1)}, f32[128]{0:T(128)S(1)}) all-reduce(f32[128]{0:T(128)S(1)} %get-tuple-element.317, f32[128]{0:T(128)S(1)} %get-tuple-element.318), channel_id=1, replica_groups=mesh['section'=4,'row'=2,'col'=4] {'row','col'}, use_global_device_ids=true, to_apply=%region_6.6 | all-reduce | flops 256 | bytes 2048 | tf_op jit(solution)/shard_map/while/body/eval_jaxpr/psum | solution.py:61
  855.4 14.0 %psum.35 = f32[8]{0:T(128)S(1)} all-reduce(f32[8]{0:T(128)S(1)} %fusion.16), channel_id=1, replica_groups=mesh['section'=4,'row'=2,'col'=4] {'row','col'}, use_global_device_ids=true, to_apply=%region_8.9 | all-reduce | flops 8 | bytes 64 | tf_op jit(solution)/shard_map/psum | solution.py:70
  (136 shorter events, 340.7 us)
Async XLA Ops:
  7.2 862.2 %copy-start = (f32[1,8,128,512]{3,2,1,0:T(8,128)S(1)}, f32[1,8,128,512]{3,2,1,0:T(8,128)}, u32[]{:S(2)}) copy-start(f32[1,8,128,512]{3,2,1,0:T(8,128)} %param.14) | copy-start | bytes 6291460
  10.2 48.5 %reduce-scatter.3.cloned.1.call-start = ((), (), s32[]{:S(2)}) async-start(), calls=%async_computation.2 | async-start | bytes 2752512 | tf_op jit(solution)/shard_map/while/body/eval_jaxpr/reduce_scatter | solution.py:40
  10.2 9.9 %collective-permute-start = (f32[128,512]{1,0:T(8,128)}, f32[128,512]{1,0:T(8,128)S(1)}, u32[]{:S(2)}, u32[]{:S(2)}) collective-permute-start(f32[128,512]{1,0:T(8,128)} %get-tuple-element.343), channel_id=1, source_target_pairs={{0,24},{8,0},{16,8},{24,16},{1,25},{9,1},{17,9},{25,17},{2,26},{10... | collective-permute-start | bytes 786440 | tf_op jit(solution)/shard_map/while/body/eval_jaxpr/ppermute | solution.py:12
  46.6 68.5 %reduce-scatter.5.cloned.1.call-start = ((), (), s32[]{:S(2)}) async-start(), calls=%async_computation.3 | async-start | bytes 1310720 | tf_op jit(solution)/shard_map/while/body/eval_jaxpr/reduce_scatter | solution.py:58
  75.4 39.7 %copy-start.2 = (f32[1,512]{1,0:T(1,128)S(1)}, f32[1,512]{1,0:T(1,128)}, u32[]{:S(2)}) copy-start(f32[1,512]{1,0:T(1,128)} %get-tuple-element.364) | copy-start | bytes 6148 | tf_op jit(solution)/shard_map/while
  131.7 45.6 %reduce-scatter.3.cloned.1.call-start = ((), (), s32[]{:S(2)}) async-start(), calls=%async_computation.2 | async-start | bytes 2752512 | tf_op jit(solution)/shard_map/while/body/eval_jaxpr/reduce_scatter | solution.py:40
  131.7 9.4 %collective-permute-start = (f32[128,512]{1,0:T(8,128)}, f32[128,512]{1,0:T(8,128)S(1)}, u32[]{:S(2)}, u32[]{:S(2)}) collective-permute-start(f32[128,512]{1,0:T(8,128)} %get-tuple-element.343), channel_id=1, source_target_pairs={{0,24},{8,0},{16,8},{24,16},{1,25},{9,1},{17,9},{25,17},{2,26},{10... | collective-permute-start | bytes 786440 | tf_op jit(solution)/shard_map/while/body/eval_jaxpr/ppermute | solution.py:12
  168.6 65.1 %reduce-scatter.5.cloned.1.call-start = ((), (), s32[]{:S(2)}) async-start(), calls=%async_computation.3 | async-start | bytes 1310720 | tf_op jit(solution)/shard_map/while/body/eval_jaxpr/reduce_scatter | solution.py:58
  194.0 39.7 %copy-start.2 = (f32[1,512]{1,0:T(1,128)S(1)}, f32[1,512]{1,0:T(1,128)}, u32[]{:S(2)}) copy-start(f32[1,512]{1,0:T(1,128)} %get-tuple-element.364) | copy-start | bytes 6148 | tf_op jit(solution)/shard_map/while
  250.3 45.6 %reduce-scatter.3.cloned.1.call-start = ((), (), s32[]{:S(2)}) async-start(), calls=%async_computation.2 | async-start | bytes 2752512 | tf_op jit(solution)/shard_map/while/body/eval_jaxpr/reduce_scatter | solution.py:40
  250.3 9.4 %collective-permute-start = (f32[128,512]{1,0:T(8,128)}, f32[128,512]{1,0:T(8,128)S(1)}, u32[]{:S(2)}, u32[]{:S(2)}) collective-permute-start(f32[128,512]{1,0:T(8,128)} %get-tuple-element.343), channel_id=1, source_target_pairs={{0,24},{8,0},{16,8},{24,16},{1,25},{9,1},{17,9},{25,17},{2,26},{10... | collective-permute-start | bytes 786440 | tf_op jit(solution)/shard_map/while/body/eval_jaxpr/ppermute | solution.py:12
  287.2 65.0 %reduce-scatter.5.cloned.1.call-start = ((), (), s32[]{:S(2)}) async-start(), calls=%async_computation.3 | async-start | bytes 1310720 | tf_op jit(solution)/shard_map/while/body/eval_jaxpr/reduce_scatter | solution.py:58
  312.6 39.7 %copy-start.2 = (f32[1,512]{1,0:T(1,128)S(1)}, f32[1,512]{1,0:T(1,128)}, u32[]{:S(2)}) copy-start(f32[1,512]{1,0:T(1,128)} %get-tuple-element.364) | copy-start | bytes 6148 | tf_op jit(solution)/shard_map/while
  368.8 45.5 %reduce-scatter.3.cloned.1.call-start = ((), (), s32[]{:S(2)}) async-start(), calls=%async_computation.2 | async-start | bytes 2752512 | tf_op jit(solution)/shard_map/while/body/eval_jaxpr/reduce_scatter | solution.py:40
  368.8 9.4 %collective-permute-start = (f32[128,512]{1,0:T(8,128)}, f32[128,512]{1,0:T(8,128)S(1)}, u32[]{:S(2)}, u32[]{:S(2)}) collective-permute-start(f32[128,512]{1,0:T(8,128)} %get-tuple-element.343), channel_id=1, source_target_pairs={{0,24},{8,0},{16,8},{24,16},{1,25},{9,1},{17,9},{25,17},{2,26},{10... | collective-permute-start | bytes 786440 | tf_op jit(solution)/shard_map/while/body/eval_jaxpr/ppermute | solution.py:12
  405.8 65.0 %reduce-scatter.5.cloned.1.call-start = ((), (), s32[]{:S(2)}) async-start(), calls=%async_computation.3 | async-start | bytes 1310720 | tf_op jit(solution)/shard_map/while/body/eval_jaxpr/reduce_scatter | solution.py:58
  431.1 39.7 %copy-start.2 = (f32[1,512]{1,0:T(1,128)S(1)}, f32[1,512]{1,0:T(1,128)}, u32[]{:S(2)}) copy-start(f32[1,512]{1,0:T(1,128)} %get-tuple-element.364) | copy-start | bytes 6148 | tf_op jit(solution)/shard_map/while
  487.4 45.5 %reduce-scatter.3.cloned.1.call-start = ((), (), s32[]{:S(2)}) async-start(), calls=%async_computation.2 | async-start | bytes 2752512 | tf_op jit(solution)/shard_map/while/body/eval_jaxpr/reduce_scatter | solution.py:40
  487.4 9.4 %collective-permute-start = (f32[128,512]{1,0:T(8,128)}, f32[128,512]{1,0:T(8,128)S(1)}, u32[]{:S(2)}, u32[]{:S(2)}) collective-permute-start(f32[128,512]{1,0:T(8,128)} %get-tuple-element.343), channel_id=1, source_target_pairs={{0,24},{8,0},{16,8},{24,16},{1,25},{9,1},{17,9},{25,17},{2,26},{10... | collective-permute-start | bytes 786440 | tf_op jit(solution)/shard_map/while/body/eval_jaxpr/ppermute | solution.py:12
  524.3 65.0 %reduce-scatter.5.cloned.1.call-start = ((), (), s32[]{:S(2)}) async-start(), calls=%async_computation.3 | async-start | bytes 1310720 | tf_op jit(solution)/shard_map/while/body/eval_jaxpr/reduce_scatter | solution.py:58
  549.6 39.7 %copy-start.2 = (f32[1,512]{1,0:T(1,128)S(1)}, f32[1,512]{1,0:T(1,128)}, u32[]{:S(2)}) copy-start(f32[1,512]{1,0:T(1,128)} %get-tuple-element.364) | copy-start | bytes 6148 | tf_op jit(solution)/shard_map/while
  605.9 45.5 %reduce-scatter.3.cloned.1.call-start = ((), (), s32[]{:S(2)}) async-start(), calls=%async_computation.2 | async-start | bytes 2752512 | tf_op jit(solution)/shard_map/while/body/eval_jaxpr/reduce_scatter | solution.py:40
  605.9 9.4 %collective-permute-start = (f32[128,512]{1,0:T(8,128)}, f32[128,512]{1,0:T(8,128)S(1)}, u32[]{:S(2)}, u32[]{:S(2)}) collective-permute-start(f32[128,512]{1,0:T(8,128)} %get-tuple-element.343), channel_id=1, source_target_pairs={{0,24},{8,0},{16,8},{24,16},{1,25},{9,1},{17,9},{25,17},{2,26},{10... | collective-permute-start | bytes 786440 | tf_op jit(solution)/shard_map/while/body/eval_jaxpr/ppermute | solution.py:12
  642.8 65.0 %reduce-scatter.5.cloned.1.call-start = ((), (), s32[]{:S(2)}) async-start(), calls=%async_computation.3 | async-start | bytes 1310720 | tf_op jit(solution)/shard_map/while/body/eval_jaxpr/reduce_scatter | solution.py:58
  668.1 39.7 %copy-start.2 = (f32[1,512]{1,0:T(1,128)S(1)}, f32[1,512]{1,0:T(1,128)}, u32[]{:S(2)}) copy-start(f32[1,512]{1,0:T(1,128)} %get-tuple-element.364) | copy-start | bytes 6148 | tf_op jit(solution)/shard_map/while
  724.4 45.5 %reduce-scatter.3.cloned.1.call-start = ((), (), s32[]{:S(2)}) async-start(), calls=%async_computation.2 | async-start | bytes 2752512 | tf_op jit(solution)/shard_map/while/body/eval_jaxpr/reduce_scatter | solution.py:40
  724.4 9.4 %collective-permute-start = (f32[128,512]{1,0:T(8,128)}, f32[128,512]{1,0:T(8,128)S(1)}, u32[]{:S(2)}, u32[]{:S(2)}) collective-permute-start(f32[128,512]{1,0:T(8,128)} %get-tuple-element.343), channel_id=1, source_target_pairs={{0,24},{8,0},{16,8},{24,16},{1,25},{9,1},{17,9},{25,17},{2,26},{10... | collective-permute-start | bytes 786440 | tf_op jit(solution)/shard_map/while/body/eval_jaxpr/ppermute | solution.py:12
  761.3 65.0 %reduce-scatter.5.cloned.1.call-start = ((), (), s32[]{:S(2)}) async-start(), calls=%async_computation.3 | async-start | bytes 1310720 | tf_op jit(solution)/shard_map/while/body/eval_jaxpr/reduce_scatter | solution.py:58
  786.6 39.7 %copy-start.2 = (f32[1,512]{1,0:T(1,128)S(1)}, f32[1,512]{1,0:T(1,128)}, u32[]{:S(2)}) copy-start(f32[1,512]{1,0:T(1,128)} %get-tuple-element.364) | copy-start | bytes 6148 | tf_op jit(solution)/shard_map/while
  842.9 9.4 %collective-permute-start.1 = (f32[128,512]{1,0:T(8,128)}, f32[128,512]{1,0:T(8,128)S(1)}, u32[]{:S(2)}, u32[]{:S(2)}) collective-permute-start(f32[128,512]{1,0:T(8,128)} %get-tuple-element.223), channel_id=1, source_target_pairs={{0,24},{8,0},{16,8},{24,16},{1,25},{9,1},{17,9},{25,17},{2,26},{10... | collective-permute-start | bytes 786440 | tf_op jit(solution)/shard_map/ppermute | solution.py:12
  853.4 20.6 %copy-start.1 = (f32[128,512]{1,0:T(8,128)}, f32[128,512]{1,0:T(8,128)S(1)}, u32[]{:S(2)}) copy-start(f32[128,512]{1,0:T(8,128)S(1)} %fusion.20) | copy-start | bytes 786436
Sparse Core Ops, SparseCore 0:
  46.7 11.8 reduce-scatter.2
  86.5 28.5 reduce-scatter.4
  168.7 8.5 reduce-scatter.2
  205.1 28.5 reduce-scatter.4
  287.3 8.4 reduce-scatter.2
  323.6 28.5 reduce-scatter.4
  405.9 8.4 reduce-scatter.2
  442.2 28.5 reduce-scatter.4
  524.4 8.4 reduce-scatter.2
  560.7 28.5 reduce-scatter.4
  642.9 8.4 reduce-scatter.2
  679.2 28.5 reduce-scatter.4
  761.5 8.4 reduce-scatter.2
  797.7 28.5 reduce-scatter.4
where the time goes:
time: 882 us; the launch traced here: 881 us
  waiting for transfers between devices  319 us (36%)
  blocking collectives  256 us (29%)
  matrix products  228 us (26%)
  other arithmetic  39.4 us (4%)
  starting transfers between devices  21 us (2%)
  between operations  13.7 us (2%)
    reduce_scatter x7, waiting for transfers between devices, layer_step(): lax.psum_scatter(first + second, 'col', scatter_dimension=0, tiled=True)  201 us
    all_gather x7, blocking collectives, layer_step(): wide = lax.all_gather(gy, 'col', axis=1, tiled=True)  112 us
    psum x7, blocking collectives, layer_step(): inner = lax.psum(jnp.sum(scaled * xf, axis=1), ('row', 'col'))[:, None] / D  95.9 us
    dot_general x7, matrix products, layer_step(): lax.dot_general(wide, wd, (((1,), (1,)), ((), ())), preferred_element_typ...  79.4 us
    dot_general x7, matrix products, layer_step(): lax.dot_general(wu, grad_up, (((1,), (1,)), ((), ())), preferred_element_...  76.5 us
    dot_general x7, matrix products, layer_step(): lax.dot_general(wg, grad_gate, (((1,), (1,)), ((), ())), preferred_elemen...  69.4 us
    reduce_scatter x7, waiting for transfers between devices, layer_step(): ga = lax.psum_scatter(ga_part, 'row', scatter_dimension=1, tiled=True)  63.1 us
    ppermute x8, waiting for transfers between devices, shifted(): lax.ppermute(x, axis, [(i, (i + by) % devices) for i in range(devices)])  54.8 us
  transfers between devices with their start and end apart: 22, of which 22 were waited for; matrix products, arithmetic and copies ran while one was open for 0% of the time, Pallas kernels for 0%

commit v1 on v0

--- a/solution.py
+++ b/solution.py
@@ -1,3 +1,4 @@
+import functools
 import jax
 import jax.numpy as jnp
 from jax import lax
@@ -5,6 +6,14 @@
 
 D = 4096
 eps = 1e-05
+
+
+def recast_shards_on_mesh(patch, mesh_ax, named_axis):
+    left_arr = lax.psum(lax.psum(patch, axis_name=mesh_ax), axis_name=named_axis)
+    return left_arr
+
+
+state_bars = functools.partial(recast_shards_on_mesh, mesh_ax="col", named_axis="row")
 
 
 def shifted(x, axis, by):
@@ -58,7 +67,7 @@
         normgrad = lax.psum_scatter(first + second, "col", scatter_dimension=0, tiled=True).T
         rstd = lax.rsqrt(sumsq / D + eps)[:, None]
         scaled = gain * normgrad
-        inner = lax.psum(jnp.sum(scaled * xf, axis=1), ("row", "col"))[:, None] / D
+        inner = state_bars(jnp.sum(scaled * xf, axis=1))[:, None] / D
         updated = carry + rstd * scaled - xf * (rstd * rstd * rstd) * inner
         active = jnp.logical_and(step >= micro, step - micro < sections)
         return jnp.where(active, updated, carry)

time: 882 us -> 965 us (1.094)
  blocking collectives: 256 us -> 344 us
    psum x7 -> x21, blocking collectives: 95.9 us -> 185 us  [the longest x7 103 us: layer_step(): sumsq = lax.psum(jnp.sum(xf * xf, axis=1), ('row', 'col'))]
where the time goes in v1:
time: 965 us; the launch traced here: 963 us
  blocking collectives  344 us (36%)
  waiting for transfers between devices  314 us (33%)
  matrix products  228 us (24%)
  other arithmetic  39.5 us (4%)
  starting transfers between devices  20.9 us (2%)
  between operations  13.7 us (1%)
    reduce_scatter x7, waiting for transfers between devices, layer_step(): lax.psum_scatter(first + second, 'col', scatter_dimension=0, tiled=True)  201 us
    all_gather x7, blocking collectives, layer_step(): wide = lax.all_gather(gy, 'col', axis=1, tiled=True)  110 us
    psum x7, blocking collectives, layer_step(): sumsq = lax.psum(jnp.sum(xf * xf, axis=1), ('row', 'col'))  103 us
    dot_general x7, matrix products, layer_step(): lax.dot_general(wide, wd, (((1,), (1,)), ((), ())), preferred_element_typ...  79.4 us
    dot_general x7, matrix products, layer_step(): lax.dot_general(wu, grad_up, (((1,), (1,)), ((), ())), preferred_element_...  76.5 us
    dot_general x7, matrix products, layer_step(): lax.dot_general(wg, grad_gate, (((1,), (1,)), ((), ())), preferred_elemen...  69.4 us
    psum x7, blocking collectives, recast_shards_on_mesh(): lax.psum(patch, axis_name=mesh_ax)  64.8 us
    reduce_scatter x7, waiting for transfers between devices, layer_step(): ga = lax.psum_scatter(ga_part, 'row', scatter_dimension=1, tiled=True)  63.7 us
  transfers between devices with their start and end apart: 22, of which 22 were waited for; matrix products, arithmetic and copies ran while one was open for 0% of the time, Pallas kernels for 0%

profile of v1, /device:TPU:0, one launch (start us, length us, event | category | flops | bytes accessed | tf_op | source)
XLA Modules:
  0.0 963.2 jit_solution(9774656558475188289)
XLA Ops:
  10.2 916.1 %while.15 = (s32[]{:T(128)}, f32[128,512]{1,0:T(8,128)}, s32[]{:T(128)}, f32[4,128,512]{2,1,0:T(8,128)S(1)}, f32[1,512]{1,0:T(1,128)}, /*index=5*/bf16[3584,2048...) while((s32[]{:T(128)}, f32[128,512]{1,0:T(8,128)}, ...), condition=%wide.region_8.9_spmd, body=%wide.region_0.8_spmd.sunk | while | flops 5641699840 | bytes 72766056 | solution.py:75
  20.1 15.1 %all_gather.33 = bf16[128,2048]{1,0:T(8,128)(2,1)S(1)} all-gather(bf16[128,512]{1,0:T(8,128)(2,1)S(1)} %convert_element_type.72), channel_id=1, replica_groups=mesh['section'=4,'row'=2,'col'=4] {'col'}, dimensions={1}, use_global_device_ids=true | all-gather | bytes 655360 | tf_op jit(solution)/shard_map/while/body/eval_jaxpr/all_gather | solution.py:45
  35.3 11.4 %fusion.48 = f32[128,3584]{1,0:T(8,128)} fusion(bf16[128,2048]{1,0:T(8,128)(2,1)S(1)} %all_gather.33, bf16[3584,2048]{1,0:T(8,128)(2,1)} %get-tuple-element.356), kind=kOutput, calls=%fused_computation.40.clone.1 | convolution fusion | flops 1879048192 | bytes 17039360 | tf_op jit(solution)/shard_map/while/body/eval_jaxpr/dot_general | solution.py:46
  46.7 12.0 %reduce-scatter.3.cloned.1.call-done = f32[128,1792]{1,0:T(8,128)} async-done(((f32[128,3584]{1,0:T(8,128)}), f32[128,1792]{1,0:T(8,128)}) %reduce-scatter.3.cloned.1.call-update) | async-done | bytes 917520 | tf_op jit(solution)/shard_map/while/body/eval_jaxpr/reduce_scatter | solution.py:49
  86.4 28.7 %reduce-scatter.5.cloned.1.call-done = f32[512,128]{0,1:T(8,128)} async-done(((f32[2048,128]{0,1:T(8,128)}), f32[512,128]{0,1:T(8,128)}) %reduce-scatter.5.cloned.1.call-update) | async-done | bytes 262160 | tf_op jit(solution)/shard_map/while/body/eval_jaxpr/reduce_scatter | solution.py:67
  127.9 14.7 %psum.55 = f32[128]{0:T(128)S(1)} all-reduce(f32[128]{0:T(128)S(1)} %get-tuple-element.312), channel_id=1, replica_groups=mesh['section'=4,'row'=2,'col'=4] {'row','col'}, use_global_device_ids=true, to_apply=%region_2.2 | all-reduce | flops 128 | bytes 1024 | tf_op jit(solution)/shard_map/while/body/eval_jaxpr/psum | solution.py:43
  153.1 15.8 %all_gather.33 = bf16[128,2048]{1,0:T(8,128)(2,1)S(1)} all-gather(bf16[128,512]{1,0:T(8,128)(2,1)S(1)} %convert_element_type.72), channel_id=1, replica_groups=mesh['section'=4,'row'=2,'col'=4] {'col'}, dimensions={1}, use_global_device_ids=true | all-gather | bytes 655360 | tf_op jit(solution)/shard_map/while/body/eval_jaxpr/all_gather | solution.py:45
  168.9 11.3 %fusion.48 = f32[128,3584]{1,0:T(8,128)} fusion(bf16[128,2048]{1,0:T(8,128)(2,1)S(1)} %all_gather.33, bf16[3584,2048]{1,0:T(8,128)(2,1)} %get-tuple-element.356), kind=kOutput, calls=%fused_computation.40.clone.1 | convolution fusion | flops 1879048192 | bytes 17039360 | tf_op jit(solution)/shard_map/while/body/eval_jaxpr/dot_general | solution.py:46
  216.7 28.7 %reduce-scatter.5.cloned.1.call-done = f32[512,128]{0,1:T(8,128)} async-done(((f32[2048,128]{0,1:T(8,128)}), f32[512,128]{0,1:T(8,128)}) %reduce-scatter.5.cloned.1.call-update) | async-done | bytes 262160 | tf_op jit(solution)/shard_map/while/body/eval_jaxpr/reduce_scatter | solution.py:67
  258.2 14.7 %psum.55 = f32[128]{0:T(128)S(1)} all-reduce(f32[128]{0:T(128)S(1)} %get-tuple-element.312), channel_id=1, replica_groups=mesh['section'=4,'row'=2,'col'=4] {'row','col'}, use_global_device_ids=true, to_apply=%region_2.2 | all-reduce | flops 128 | bytes 1024 | tf_op jit(solution)/shard_map/while/body/eval_jaxpr/psum | solution.py:43
  283.4 15.9 %all_gather.33 = bf16[128,2048]{1,0:T(8,128)(2,1)S(1)} all-gather(bf16[128,512]{1,0:T(8,128)(2,1)S(1)} %convert_element_type.72), channel_id=1, replica_groups=mesh['section'=4,'row'=2,'col'=4] {'col'}, dimensions={1}, use_global_device_ids=true | all-gather | bytes 655360 | tf_op jit(solution)/shard_map/while/body/eval_jaxpr/all_gather | solution.py:45
  299.2 11.4 %fusion.48 = f32[128,3584]{1,0:T(8,128)} fusion(bf16[128,2048]{1,0:T(8,128)(2,1)S(1)} %all_gather.33, bf16[3584,2048]{1,0:T(8,128)(2,1)} %get-tuple-element.356), kind=kOutput, calls=%fused_computation.40.clone.1 | convolution fusion | flops 1879048192 | bytes 17039360 | tf_op jit(solution)/shard_map/while/body/eval_jaxpr/dot_general | solution.py:46
  347.0 28.7 %reduce-scatter.5.cloned.1.call-done = f32[512,128]{0,1:T(8,128)} async-done(((f32[2048,128]{0,1:T(8,128)}), f32[512,128]{0,1:T(8,128)}) %reduce-scatter.5.cloned.1.call-update) | async-done | bytes 262160 | tf_op jit(solution)/shard_map/while/body/eval_jaxpr/reduce_scatter | solution.py:67
  388.5 14.7 %psum.55 = f32[128]{0:T(128)S(1)} all-reduce(f32[128]{0:T(128)S(1)} %get-tuple-element.312), channel_id=1, replica_groups=mesh['section'=4,'row'=2,'col'=4] {'row','col'}, use_global_device_ids=true, to_apply=%region_2.2 | all-reduce | flops 128 | bytes 1024 | tf_op jit(solution)/shard_map/while/body/eval_jaxpr/psum | solution.py:43
  413.7 15.8 %all_gather.33 = bf16[128,2048]{1,0:T(8,128)(2,1)S(1)} all-gather(bf16[128,512]{1,0:T(8,128)(2,1)S(1)} %convert_element_type.72), channel_id=1, replica_groups=mesh['section'=4,'row'=2,'col'=4] {'col'}, dimensions={1}, use_global_device_ids=true | all-gather | bytes 655360 | tf_op jit(solution)/shard_map/while/body/eval_jaxpr/all_gather | solution.py:45
  429.5 11.3 %fusion.48 = f32[128,3584]{1,0:T(8,128)} fusion(bf16[128,2048]{1,0:T(8,128)(2,1)S(1)} %all_gather.33, bf16[3584,2048]{1,0:T(8,128)(2,1)} %get-tuple-element.356), kind=kOutput, calls=%fused_computation.40.clone.1 | convolution fusion | flops 1879048192 | bytes 17039360 | tf_op jit(solution)/shard_map/while/body/eval_jaxpr/dot_general | solution.py:46
  477.3 28.7 %reduce-scatter.5.cloned.1.call-done = f32[512,128]{0,1:T(8,128)} async-done(((f32[2048,128]{0,1:T(8,128)}), f32[512,128]{0,1:T(8,128)}) %reduce-scatter.5.cloned.1.call-update) | async-done | bytes 262160 | tf_op jit(solution)/shard_map/while/body/eval_jaxpr/reduce_scatter | solution.py:67
  518.8 14.7 %psum.55 = f32[128]{0:T(128)S(1)} all-reduce(f32[128]{0:T(128)S(1)} %get-tuple-element.312), channel_id=1, replica_groups=mesh['section'=4,'row'=2,'col'=4] {'row','col'}, use_global_device_ids=true, to_apply=%region_2.2 | all-reduce | flops 128 | bytes 1024 | tf_op jit(solution)/shard_map/while/body/eval_jaxpr/psum | solution.py:43
  544.0 15.8 %all_gather.33 = bf16[128,2048]{1,0:T(8,128)(2,1)S(1)} all-gather(bf16[128,512]{1,0:T(8,128)(2,1)S(1)} %convert_element_type.72), channel_id=1, replica_groups=mesh['section'=4,'row'=2,'col'=4] {'col'}, dimensions={1}, use_global_device_ids=true | all-gather | bytes 655360 | tf_op jit(solution)/shard_map/while/body/eval_jaxpr/all_gather | solution.py:45
  559.8 11.3 %fusion.48 = f32[128,3584]{1,0:T(8,128)} fusion(bf16[128,2048]{1,0:T(8,128)(2,1)S(1)} %all_gather.33, bf16[3584,2048]{1,0:T(8,128)(2,1)} %get-tuple-element.356), kind=kOutput, calls=%fused_computation.40.clone.1 | convolution fusion | flops 1879048192 | bytes 17039360 | tf_op jit(solution)/shard_map/while/body/eval_jaxpr/dot_general | solution.py:46
  607.6 28.7 %reduce-scatter.5.cloned.1.call-done = f32[512,128]{0,1:T(8,128)} async-done(((f32[2048,128]{0,1:T(8,128)}), f32[512,128]{0,1:T(8,128)}) %reduce-scatter.5.cloned.1.call-update) | async-done | bytes 262160 | tf_op jit(solution)/shard_map/while/body/eval_jaxpr/reduce_scatter | solution.py:67
  649.1 14.7 %psum.55 = f32[128]{0:T(128)S(1)} all-reduce(f32[128]{0:T(128)S(1)} %get-tuple-element.312), channel_id=1, replica_groups=mesh['section'=4,'row'=2,'col'=4] {'row','col'}, use_global_device_ids=true, to_apply=%region_2.2 | all-reduce | flops 128 | bytes 1024 | tf_op jit(solution)/shard_map/while/body/eval_jaxpr/psum | solution.py:43
  674.3 15.8 %all_gather.33 = bf16[128,2048]{1,0:T(8,128)(2,1)S(1)} all-gather(bf16[128,512]{1,0:T(8,128)(2,1)S(1)} %convert_element_type.72), channel_id=1, replica_groups=mesh['section'=4,'row'=2,'col'=4] {'col'}, dimensions={1}, use_global_device_ids=true | all-gather | bytes 655360 | tf_op jit(solution)/shard_map/while/body/eval_jaxpr/all_gather | solution.py:45
  690.1 11.3 %fusion.48 = f32[128,3584]{1,0:T(8,128)} fusion(bf16[128,2048]{1,0:T(8,128)(2,1)S(1)} %all_gather.33, bf16[3584,2048]{1,0:T(8,128)(2,1)} %get-tuple-element.356), kind=kOutput, calls=%fused_computation.40.clone.1 | convolution fusion | flops 1879048192 | bytes 17039360 | tf_op jit(solution)/shard_map/while/body/eval_jaxpr/dot_general | solution.py:46
  737.9 28.7 %reduce-scatter.5.cloned.1.call-done = f32[512,128]{0,1:T(8,128)} async-done(((f32[2048,128]{0,1:T(8,128)}), f32[512,128]{0,1:T(8,128)}) %reduce-scatter.5.cloned.1.call-update) | async-done | bytes 262160 | tf_op jit(solution)/shard_map/while/body/eval_jaxpr/reduce_scatter | solution.py:67
  779.4 14.7 %psum.55 = f32[128]{0:T(128)S(1)} all-reduce(f32[128]{0:T(128)S(1)} %get-tuple-element.312), channel_id=1, replica_groups=mesh['section'=4,'row'=2,'col'=4] {'row','col'}, use_global_device_ids=true, to_apply=%region_2.2 | all-reduce | flops 128 | bytes 1024 | tf_op jit(solution)/shard_map/while/body/eval_jaxpr/psum | solution.py:43
  804.6 15.8 %all_gather.33 = bf16[128,2048]{1,0:T(8,128)(2,1)S(1)} all-gather(bf16[128,512]{1,0:T(8,128)(2,1)S(1)} %convert_element_type.72), channel_id=1, replica_groups=mesh['section'=4,'row'=2,'col'=4] {'col'}, dimensions={1}, use_global_device_ids=true | all-gather | bytes 655360 | tf_op jit(solution)/shard_map/while/body/eval_jaxpr/all_gather | solution.py:45
  820.4 11.3 %fusion.48 = f32[128,3584]{1,0:T(8,128)} fusion(bf16[128,2048]{1,0:T(8,128)(2,1)S(1)} %all_gather.33, bf16[3584,2048]{1,0:T(8,128)(2,1)} %get-tuple-element.356), kind=kOutput, calls=%fused_computation.40.clone.1 | convolution fusion | flops 1879048192 | bytes 17039360 | tf_op jit(solution)/shard_map/while/body/eval_jaxpr/dot_general | solution.py:46
  857.2 10.9 %fusion.51 = f32[2048,128]{0,1:T(8,128)} fusion(f32[128,2048]{1,0:T(8,128)S(1)} %fusion.50, bf16[128,3584]{1,0:T(8,128)(2,1)S(1)} %all_gather.35, bf16[2048,3584]{1,0:T(8,128)(2,1)} %get-tuple-element.359), kind=kOutput, calls=%fused_computation.1.clone.1 | convolution fusion | flops 1879310336 | bytes 17694720 | tf_op jit(solution)/shard_map/while/body/eval_jaxpr/dot_general | solution.py:64
  868.2 28.7 %reduce-scatter.5.cloned.1.call-done = f32[512,128]{0,1:T(8,128)} async-done(((f32[2048,128]{0,1:T(8,128)}), f32[512,128]{0,1:T(8,128)}) %reduce-scatter.5.cloned.1.call-update) | async-done | bytes 262160 | tf_op jit(solution)/shard_map/while/body/eval_jaxpr/reduce_scatter | solution.py:67
  909.7 14.7 %psum.55 = f32[128]{0:T(128)S(1)} all-reduce(f32[128]{0:T(128)S(1)} %get-tuple-element.312), channel_id=1, replica_groups=mesh['section'=4,'row'=2,'col'=4] {'row','col'}, use_global_device_ids=true, to_apply=%region_2.2 | all-reduce | flops 128 | bytes 1024 | tf_op jit(solution)/shard_map/while/body/eval_jaxpr/psum | solution.py:43
  937.9 14.2 %psum.49 = f32[8]{0:T(128)S(1)} all-reduce(f32[8]{0:T(128)S(1)} %fusion.16), channel_id=1, replica_groups=mesh['section'=4,'row'=2,'col'=4] {'row','col'}, use_global_device_ids=true, to_apply=%region_9.10 | all-reduce | flops 8 | bytes 64 | tf_op jit(solution)/shard_map/psum | solution.py:79
  (157 shorter events, 417.9 us)
Async XLA Ops:
  7.2 944.9 %copy-start = (f32[1,8,128,512]{3,2,1,0:T(8,128)S(1)}, f32[1,8,128,512]{3,2,1,0:T(8,128)}, u32[]{:S(2)}) copy-start(f32[1,8,128,512]{3,2,1,0:T(8,128)} %param.14) | copy-start | bytes 6291460
  10.2 48.5 %reduce-scatter.3.cloned.1.call-start = ((), (), s32[]{:S(2)}) async-start(), calls=%async_computation.2 | async-start | bytes 2752512 | tf_op jit(solution)/shard_map/while/body/eval_jaxpr/reduce_scatter | solution.py:49
  10.2 9.9 %collective-permute-start = (f32[128,512]{1,0:T(8,128)}, f32[128,512]{1,0:T(8,128)S(1)}, u32[]{:S(2)}, u32[]{:S(2)}) collective-permute-start(f32[128,512]{1,0:T(8,128)} %get-tuple-element.334), channel_id=1, source_target_pairs={{0,24},{8,0},{16,8},{24,16},{1,25},{9,1},{17,9},{25,17},{2,26},{10... | collective-permute-start | bytes 786440 | tf_op jit(solution)/shard_map/while/body/eval_jaxpr/ppermute | solution.py:21
  46.6 68.5 %reduce-scatter.5.cloned.1.call-start = ((), (), s32[]{:S(2)}) async-start(), calls=%async_computation.3 | async-start | bytes 1310720 | tf_op jit(solution)/shard_map/while/body/eval_jaxpr/reduce_scatter | solution.py:67
  75.4 39.7 %copy-start.2 = (f32[1,512]{1,0:T(1,128)S(1)}, f32[1,512]{1,0:T(1,128)}, u32[]{:S(2)}) copy-start(f32[1,512]{1,0:T(1,128)} %get-tuple-element.355) | copy-start | bytes 6148 | tf_op jit(solution)/shard_map/while
  144.4 44.6 %reduce-scatter.3.cloned.1.call-start = ((), (), s32[]{:S(2)}) async-start(), calls=%async_computation.2 | async-start | bytes 2752512 | tf_op jit(solution)/shard_map/while/body/eval_jaxpr/reduce_scatter | solution.py:49
  144.4 8.6 collective-permute-start
  180.3 65.1 %reduce-scatter.5.cloned.1.call-start = ((), (), s32[]{:S(2)}) async-start(), calls=%async_computation.3 | async-start | bytes 1310720 | tf_op jit(solution)/shard_map/while/body/eval_jaxpr/reduce_scatter | solution.py:67
  205.7 39.7 %copy-start.2 = (f32[1,512]{1,0:T(1,128)S(1)}, f32[1,512]{1,0:T(1,128)}, u32[]{:S(2)}) copy-start(f32[1,512]{1,0:T(1,128)} %get-tuple-element.355) | copy-start | bytes 6148 | tf_op jit(solution)/shard_map/while
  274.8 44.5 %reduce-scatter.3.cloned.1.call-start = ((), (), s32[]{:S(2)}) async-start(), calls=%async_computation.2 | async-start | bytes 2752512 | tf_op jit(solution)/shard_map/while/body/eval_jaxpr/reduce_scatter | solution.py:49
  274.8 8.6 collective-permute-start
  310.6 65.1 %reduce-scatter.5.cloned.1.call-start = ((), (), s32[]{:S(2)}) async-start(), calls=%async_computation.3 | async-start | bytes 1310720 | tf_op jit(solution)/shard_map/while/body/eval_jaxpr/reduce_scatter | solution.py:67
  336.0 39.7 %copy-start.2 = (f32[1,512]{1,0:T(1,128)S(1)}, f32[1,512]{1,0:T(1,128)}, u32[]{:S(2)}) copy-start(f32[1,512]{1,0:T(1,128)} %get-tuple-element.355) | copy-start | bytes 6148 | tf_op jit(solution)/shard_map/while
  405.1 44.5 %reduce-scatter.3.cloned.1.call-start = ((), (), s32[]{:S(2)}) async-start(), calls=%async_computation.2 | async-start | bytes 2752512 | tf_op jit(solution)/shard_map/while/body/eval_jaxpr/reduce_scatter | solution.py:49
  405.1 8.6 collective-permute-start
  440.9 65.1 %reduce-scatter.5.cloned.1.call-start = ((), (), s32[]{:S(2)}) async-start(), calls=%async_computation.3 | async-start | bytes 1310720 | tf_op jit(solution)/shard_map/while/body/eval_jaxpr/reduce_scatter | solution.py:67
  466.3 39.7 %copy-start.2 = (f32[1,512]{1,0:T(1,128)S(1)}, f32[1,512]{1,0:T(1,128)}, u32[]{:S(2)}) copy-start(f32[1,512]{1,0:T(1,128)} %get-tuple-element.355) | copy-start | bytes 6148 | tf_op jit(solution)/shard_map/while
  535.4 44.5 %reduce-scatter.3.cloned.1.call-start = ((), (), s32[]{:S(2)}) async-start(), calls=%async_computation.2 | async-start | bytes 2752512 | tf_op jit(solution)/shard_map/while/body/eval_jaxpr/reduce_scatter | solution.py:49
  535.4 8.6 collective-permute-start
  571.2 65.1 %reduce-scatter.5.cloned.1.call-start = ((), (), s32[]{:S(2)}) async-start(), calls=%async_computation.3 | async-start | bytes 1310720 | tf_op jit(solution)/shard_map/while/body/eval_jaxpr/reduce_scatter | solution.py:67
  596.6 39.7 %copy-start.2 = (f32[1,512]{1,0:T(1,128)S(1)}, f32[1,512]{1,0:T(1,128)}, u32[]{:S(2)}) copy-start(f32[1,512]{1,0:T(1,128)} %get-tuple-element.355) | copy-start | bytes 6148 | tf_op jit(solution)/shard_map/while
  665.7 44.5 %reduce-scatter.3.cloned.1.call-start = ((), (), s32[]{:S(2)}) async-start(), calls=%async_computation.2 | async-start | bytes 2752512 | tf_op jit(solution)/shard_map/while/body/eval_jaxpr/reduce_scatter | solution.py:49
  665.7 8.6 collective-permute-start
  701.5 65.1 %reduce-scatter.5.cloned.1.call-start = ((), (), s32[]{:S(2)}) async-start(), calls=%async_computation.3 | async-start | bytes 1310720 | tf_op jit(solution)/shard_map/while/body/eval_jaxpr/reduce_scatter | solution.py:67
  726.9 39.7 %copy-start.2 = (f32[1,512]{1,0:T(1,128)S(1)}, f32[1,512]{1,0:T(1,128)}, u32[]{:S(2)}) copy-start(f32[1,512]{1,0:T(1,128)} %get-tuple-element.355) | copy-start | bytes 6148 | tf_op jit(solution)/shard_map/while
  796.0 44.5 %reduce-scatter.3.cloned.1.call-start = ((), (), s32[]{:S(2)}) async-start(), calls=%async_computation.2 | async-start | bytes 2752512 | tf_op jit(solution)/shard_map/while/body/eval_jaxpr/reduce_scatter | solution.py:49
  796.0 8.6 collective-permute-start
  831.8 65.1 %reduce-scatter.5.cloned.1.call-start = ((), (), s32[]{:S(2)}) async-start(), calls=%async_computation.3 | async-start | bytes 1310720 | tf_op jit(solution)/shard_map/while/body/eval_jaxpr/reduce_scatter | solution.py:67
  857.2 39.7 %copy-start.2 = (f32[1,512]{1,0:T(1,128)S(1)}, f32[1,512]{1,0:T(1,128)}, u32[]{:S(2)}) copy-start(f32[1,512]{1,0:T(1,128)} %get-tuple-element.355) | copy-start | bytes 6148 | tf_op jit(solution)/shard_map/while
  926.3 8.6 collective-permute-start.1
  936.0 20.7 %copy-start.1 = (f32[128,512]{1,0:T(8,128)}, f32[128,512]{1,0:T(8,128)S(1)}, u32[]{:S(2)}) copy-start(f32[128,512]{1,0:T(8,128)S(1)} %fusion.20) | copy-start | bytes 786436
Sparse Core Ops, SparseCore 0:
  46.7 11.8 reduce-scatter.2
  86.5 28.5 reduce-scatter.4
  180.4 8.5 reduce-scatter.2
  216.8 28.5 reduce-scatter.4
  310.7 8.5 reduce-scatter.2
  347.1 28.5 reduce-scatter.4
  441.0 8.5 reduce-scatter.2
  477.4 28.5 reduce-scatter.4
  571.3 8.5 reduce-scatter.2
  607.7 28.5 reduce-scatter.4
  701.6 8.5 reduce-scatter.2
  738.0 28.5 reduce-scatter.4
  831.9 8.5 reduce-scatter.2
  868.3 28.5 reduce-scatter.4
